TPU v7x, 128 devices: a whole 4x4x4 slice. The times are simulated.
128 devices in a mesh: row: 16 (over y, z), col: 8 (over x, core).
Axes of the slice: x: 4, y: 4, z: 4, core: 2. Of those that a mesh axis runs over, the one named last changes fastest.
Arguments:
- fock_matrix: bfloat16 [3072, 3072], P('row', 'col'), as said below
- density: bfloat16 [3072, 3072], P('row', 'col'), as said below
- margin: bfloat16 [3072, 3072], P('row', 'col'), as said below
- fill_patterns: int32 [3, 96, 96], P(None, 'row', 'col'), may hold values from 0 to 1, as said below
- first_filters: int32 [3, 96, 96], P(None, 'row', 'col'), may hold values from 0 to 1, as said below
- owner_order: int32 [96], replicated, may hold values from 0 to 95, as said below
- second_filters: int32 [7, 96, 96], P(None, 'row', 'col'), may hold values from 0 to 1, as said below
Outputs:
- evolved: bfloat16 [3072, 3072], P('row', 'col')
Inputs may be any that keep to these rules, and one draw needn't show every extreme that they name: `fock_matrix`: Symmetric. `density`: Symmetric. `margin`: Symmetric, with unit diagonal. `fill_patterns`: each entry says whether a block is kept; each pattern is symmetric and keeps every diagonal block. `first_filters`: each entry says whether a block of the product is kept; each filter is symmetric and keeps every diagonal block. `second_filters`: each entry says whether a block of the product is kept, indexed in owner order; each filter is symmetric and keeps every diagonal block. `owner_order`: A permutation of the 96 block indices.
All inputs are finite; a program needn't handle non-finite values.
Results may differ from a plain program's by a relative error of at most 0.012.
Values may be sent and summed in bfloat16 or wider, within the bound.
A program may use at most 64 MiB of HBM per device.

v0:
```python
import jax
import jax.numpy as jnp
from jax import lax
from jax.sharding import PartitionSpec as P

BLK = 32
TERMS = 6
SQUARINGS = 2


def expand(mask, values):
    row_blocks = mask.shape[0]
    column_blocks = mask.shape[1]
    shaped = values.reshape(row_blocks, BLK, column_blocks, BLK) * mask[:, None, :, None].astype(
        values.dtype
    )
    return shaped.reshape(values.shape)


def panel_rows(matrix):
    return lax.all_gather(matrix, "col", axis=1, tiled=True)


def panel_times(row_panel, matrix):
    return jnp.dot(
        row_panel,
        lax.all_gather(matrix, "row", axis=0, tiled=True),
        preferred_element_type=jnp.float32,
    )


def reorder(generator, owner_order):
    row_blocks = generator.shape[0] // BLK
    column_blocks = generator.shape[1] // BLK
    wanted_rows = lax.dynamic_slice_in_dim(
        owner_order, lax.axis_index("row") * row_blocks, row_blocks
    )
    wanted_columns = lax.dynamic_slice_in_dim(
        owner_order, lax.axis_index("col") * column_blocks, column_blocks
    )
    segment = lax.all_gather(generator, "row", axis=0, tiled=True)
    arriving = segment.shape[0] // BLK
    source = jnp.arange(arriving, dtype=jnp.int32)
    select = (wanted_rows[:, None] == source[None, :]).astype(jnp.bfloat16)
    flattened = segment.reshape(arriving, -1)
    by_rows = jnp.dot(select, flattened, preferred_element_type=jnp.float32)
    by_rows = by_rows.reshape(generator.shape).astype(jnp.bfloat16)
    segment = lax.all_gather(by_rows, "col", axis=1, tiled=True)
    arriving = segment.shape[1] // BLK
    source = jnp.arange(arriving, dtype=jnp.int32)
    select = (source[:, None] == wanted_columns[None, :]).astype(jnp.bfloat16)
    shaped = segment.reshape(segment.shape[0], arriving, BLK)
    placed = jnp.einsum("pjk,ji->pik", shaped, select, preferred_element_type=jnp.float32)
    return placed.reshape(generator.shape).astype(jnp.bfloat16)


def on_device(
    fock_matrix, density, margin, fill_patterns, first_filters, owner_order, second_filters
):
    masked_fock = expand(fill_patterns[0], fock_matrix)
    masked_density = expand(fill_patterns[1], density)
    masked_margin = expand(fill_patterns[2], margin)
    fock_density = expand(
        first_filters[0], panel_times(panel_rows(masked_fock), masked_density)
    ).astype(jnp.bfloat16)
    margin_density = expand(
        first_filters[1], panel_times(panel_rows(masked_margin), masked_density)
    ).astype(jnp.bfloat16)
    generator = panel_times(panel_rows(fock_density), masked_margin) - panel_times(
        panel_rows(margin_density), masked_fock
    )
    generator = expand(first_filters[2], generator).astype(jnp.bfloat16)
    reordered = reorder(generator, owner_order)
    scaled = (reordered.astype(jnp.float32) * 0.25).astype(jnp.bfloat16)
    rows_here, columns_here = scaled.shape
    row_ids = lax.axis_index("row") * rows_here + jnp.arange(rows_here, dtype=jnp.int32)
    column_ids = lax.axis_index("col") * columns_here + jnp.arange(columns_here, dtype=jnp.int32)
    identity = (row_ids[:, None] == column_ids[None, :]).astype(jnp.float32)
    scaled_rows = panel_rows(scaled)
    series = (identity + scaled.astype(jnp.float32) / 6.0).astype(jnp.bfloat16)
    for number in range(TERMS - 1):
        degree = TERMS - 1 - number
        series = (
            identity + expand(second_filters[number], panel_times(scaled_rows, series)) / degree
        ).astype(jnp.bfloat16)
    for number in range(SQUARINGS):
        series = expand(
            second_filters[TERMS - 1 + number], panel_times(panel_rows(series), series)
        ).astype(jnp.bfloat16)
    return series


def solution(mesh):
    return jax.shard_map(
        on_device,
        mesh=mesh,
        in_specs=(
            P("row", "col"),
            P("row", "col"),
            P("row", "col"),
            P(None, "row", "col"),
            P(None, "row", "col"),
            P(),
            P(None, "row", "col"),
        ),
        out_specs=P("row", "col"),
        check_vma=False,
    )
```

profile of v0, /device:TPU:1, one launch (start us, length us, event | category | flops | bytes accessed | tf_op | source)
XLA Modules:
  0.0 755.9 jit_solution(15816942738153316803)
XLA Ops:
  12.9 23.3 %all-gather.20.cloned.1.call-done = bf16[192,3072]{1,0:T(8,128)(2,1)} async-done(((bf16[192,384]{1,0:T(8,128)(2,1)}), bf16[192,3072]{1,0:T(8,128)(2,1)}) %all-gather.20.cloned.1.call-update) | async-done | bytes 1179664 | tf_op jit(solution)/shard_map/all_gather | solution.py:21
  36.2 46.1 %all-gather.22.cloned.1.call-done = bf16[3072,384]{1,0:T(8,128)(2,1)} async-done(((bf16[192,384]{1,0:T(8,128)(2,1)}), bf16[3072,384]{1,0:T(8,128)(2,1)}) %all-gather.22.cloned.1.call-update) | async-done | bytes 2359312 | tf_op jit(solution)/shard_map/all_gather | solution.py:27
  82.3 3.5 fusion.32
  89.6 18.8 %all-gather.28.cloned.1.call-done = bf16[192,3072]{1,0:T(8,128)(2,1)} async-done(((bf16[192,384]{1,0:T(8,128)(2,1)}), bf16[192,3072]{1,0:T(8,128)(2,1)}) %all-gather.28.cloned.1.call-update) | async-done | bytes 1179664 | tf_op jit(solution)/shard_map/all_gather | solution.py:21
  108.5 2.7 fusion.33
  111.9 42.6 %all-gather.26.cloned.1.call-done = bf16[3072,384]{1,0:T(8,128)(2,1)} async-done(((bf16[192,384]{1,0:T(8,128)(2,1)}), bf16[3072,384]{1,0:T(8,128)(2,1)}) %all-gather.26.cloned.1.call-update) | async-done | bytes 2359312 | tf_op jit(solution)/shard_map/all_gather | solution.py:27
  154.5 26.0 %all-gather.24.cloned.1.call-done = bf16[192,3072]{1,0:T(8,128)(2,1)} async-done(((bf16[192,384]{1,0:T(8,128)(2,1)}), bf16[192,3072]{1,0:T(8,128)(2,1)}) %all-gather.24.cloned.1.call-update) | async-done | bytes 1179664 | tf_op jit(solution)/shard_map/all_gather | solution.py:21
  180.5 2.8 fusion.50
  183.4 43.2 %all-gather.32.cloned.1.call-done = bf16[3072,384]{1,0:T(8,128)(2,1)} async-done(((bf16[192,384]{1,0:T(8,128)(2,1)}), bf16[3072,384]{1,0:T(8,128)(2,1)}) %all-gather.32.cloned.1.call-update) | async-done | bytes 2359312 | tf_op jit(solution)/shard_map/all_gather | solution.py:27
  226.5 26.2 %all-gather.30.cloned.1.call-done = bf16[192,3072]{1,0:T(8,128)(2,1)} async-done(((bf16[192,384]{1,0:T(8,128)(2,1)}), bf16[192,3072]{1,0:T(8,128)(2,1)}) %all-gather.30.cloned.1.call-update) | async-done | bytes 1179664 | tf_op jit(solution)/shard_map/all_gather | solution.py:21
  252.7 3.5 fusion.34
  256.4 43.9 %all-gather.34.cloned.1.call-done = bf16[3072,384]{1,0:T(8,128)(2,1)} async-done(((bf16[192,384]{1,0:T(8,128)(2,1)}), bf16[3072,384]{1,0:T(8,128)(2,1)}) %all-gather.34.cloned.1.call-update) | async-done | bytes 2359312 | tf_op jit(solution)/shard_map/all_gather | solution.py:41
  300.3 3.0 reshape.167
  305.0 25.3 %all-gather.36.cloned.1.call-done = bf16[192,3072]{0,1:T(8,128)(2,1)} async-done(((bf16[192,384]{0,1:T(8,128)(2,1)}), bf16[192,3072]{0,1:T(8,128)(2,1)}) %all-gather.36.cloned.1.call-update) | async-done | bytes 1179664 | tf_op jit(solution)/shard_map/all_gather | solution.py:48
  330.3 2.4 fusion.24
  336.1 22.0 %all-gather.38.cloned.1.call-done = bf16[192,3072]{0,1:T(8,128)(2,1)} async-done(((bf16[192,384]{0,1:T(8,128)(2,1)}), bf16[192,3072]{0,1:T(8,128)(2,1)}) %all-gather.38.cloned.1.call-update) | async-done | bytes 1179664 | tf_op jit(solution)/shard_map/all_gather | solution.py:21
  358.1 46.4 %all-gather.40.cloned.1.call-done = bf16[3072,384]{1,0:T(8,128)(2,1)} async-done(((bf16[192,384]{1,0:T(8,128)(2,1)}), bf16[3072,384]{1,0:T(8,128)(2,1)}) %all-gather.40.cloned.1.call-update) | async-done | bytes 2359312 | tf_op jit(solution)/shard_map/all_gather | solution.py:27
  404.4 3.6 fusion.31
  409.0 44.2 %all-gather.42.cloned.1.call-done = bf16[3072,384]{1,0:T(8,128)(2,1)} async-done(((bf16[192,384]{1,0:T(8,128)(2,1)}), bf16[3072,384]{1,0:T(8,128)(2,1)}) %all-gather.42.cloned.1.call-update) | async-done | bytes 2359312 | tf_op jit(solution)/shard_map/all_gather | solution.py:27
  453.1 3.2 fusion.30
  457.0 44.4 %all-gather.44.cloned.1.call-done = bf16[3072,384]{1,0:T(8,128)(2,1)} async-done(((bf16[192,384]{1,0:T(8,128)(2,1)}), bf16[3072,384]{1,0:T(8,128)(2,1)}) %all-gather.44.cloned.1.call-update) | async-done | bytes 2359312 | tf_op jit(solution)/shard_map/all_gather | solution.py:27
  501.4 3.2 fusion.29
  505.3 44.4 %all-gather.46.cloned.1.call-done = bf16[3072,384]{1,0:T(8,128)(2,1)} async-done(((bf16[192,384]{1,0:T(8,128)(2,1)}), bf16[3072,384]{1,0:T(8,128)(2,1)}) %all-gather.46.cloned.1.call-update) | async-done | bytes 2359312 | tf_op jit(solution)/shard_map/all_gather | solution.py:27
  549.6 3.2 fusion.28
  553.5 44.4 %all-gather.48.cloned.1.call-done = bf16[3072,384]{1,0:T(8,128)(2,1)} async-done(((bf16[192,384]{1,0:T(8,128)(2,1)}), bf16[3072,384]{1,0:T(8,128)(2,1)}) %all-gather.48.cloned.1.call-update) | async-done | bytes 2359312 | tf_op jit(solution)/shard_map/all_gather | solution.py:27
  597.8 3.2 fusion.27
  602.3 23.3 %all-gather.50.cloned.1.call-done = bf16[192,3072]{1,0:T(8,128)(2,1)} async-done(((bf16[192,384]{1,0:T(8,128)(2,1)}), bf16[192,3072]{1,0:T(8,128)(2,1)}) %all-gather.50.cloned.1.call-update) | async-done | bytes 1179664 | tf_op jit(solution)/shard_map/all_gather | solution.py:21
  625.6 46.0 %all-gather.52.cloned.1.call-done = bf16[3072,384]{1,0:T(8,128)(2,1)} async-done(((bf16[192,384]{1,0:T(8,128)(2,1)}), bf16[3072,384]{1,0:T(8,128)(2,1)}) %all-gather.52.cloned.1.call-update) | async-done | bytes 2359312 | tf_op jit(solution)/shard_map/all_gather | solution.py:27
  671.6 3.5 fusion.35
  676.5 23.2 %all-gather.54.cloned.1.call-done = bf16[192,3072]{1,0:T(8,128)(2,1)} async-done(((bf16[192,384]{1,0:T(8,128)(2,1)}), bf16[192,3072]{1,0:T(8,128)(2,1)}) %all-gather.54.cloned.1.call-update) | async-done | bytes 1179664 | tf_op jit(solution)/shard_map/all_gather | solution.py:21
  699.8 46.1 %all-gather.56.cloned.1.call-done = bf16[3072,384]{1,0:T(8,128)(2,1)} async-done(((bf16[192,384]{1,0:T(8,128)(2,1)}), bf16[3072,384]{1,0:T(8,128)(2,1)}) %all-gather.56.cloned.1.call-update) | async-done | bytes 2359312 | tf_op jit(solution)/shard_map/all_gather | solution.py:27
  745.9 3.5 fusion.36
  (101 shorter events, 21.4 us)
Async XLA Ops:
  6.5 1.4 copy-start.1
  6.5 29.6 %all-gather.20.cloned.1.call-start = ((), (), s32[]{:S(2)}) async-start(), calls=%async_computation | async-start | bytes 1327104 | tf_op jit(solution)/shard_map/all_gather | solution.py:21
  7.5 1.9 copy-start.2
  8.7 73.6 %all-gather.22.cloned.1.call-start = ((), (), s32[]{:S(2)}) async-start(), calls=%async_computation.1 | async-start | bytes 2506752 | tf_op jit(solution)/shard_map/all_gather | solution.py:27
  8.9 1.9 copy-start.3
  9.4 2.8 copy-start.5
  10.2 98.3 %all-gather.28.cloned.1.call-start = ((), (), s32[]{:S(2)}) async-start(), calls=%async_computation.4 | async-start | bytes 1327104 | tf_op jit(solution)/shard_map/all_gather | solution.py:21
  11.6 142.9 %all-gather.26.cloned.1.call-start = ((), (), s32[]{:S(2)}) async-start(), calls=%async_computation.3 | async-start | bytes 2506752 | tf_op jit(solution)/shard_map/all_gather | solution.py:27
  12.2 168.4 %all-gather.24.cloned.1.call-start = ((), (), s32[]{:S(2)}) async-start(), calls=%async_computation.2 | async-start | bytes 1327104 | tf_op jit(solution)/shard_map/all_gather | solution.py:21
  85.8 140.8 %all-gather.32.cloned.1.call-start = ((), (), s32[]{:S(2)}) async-start(), calls=%async_computation.6 | async-start | bytes 2506752 | tf_op jit(solution)/shard_map/all_gather | solution.py:27
  86.3 166.4 %all-gather.30.cloned.1.call-start = ((), (), s32[]{:S(2)}) async-start(), calls=%async_computation.5 | async-start | bytes 1327104 | tf_op jit(solution)/shard_map/all_gather | solution.py:21
  86.4 22.1 %copy-start = (bf16[3072,384]{1,0:T(8,128)(2,1)S(1)}, bf16[3072,384]{1,0:T(8,128)(2,1)}, u32[]{:S(2)}) copy-start(bf16[3072,384]{1,0:T(8,128)(2,1)} %all-gather.22.cloned.1.call-done) | copy-start | bytes 7077892
  111.2 189.1 %all-gather.34.cloned.1.call-start = ((), (), s32[]{:S(2)}) async-start(), calls=%async_computation.7 | async-start | bytes 2506752 | tf_op jit(solution)/shard_map/all_gather | solution.py:41
  183.4 72.9 %copy-start.7 = (s32[96]{0:T(128)S(1)}, s32[96]{0:T(128)}, u32[]{:S(2)}) copy-start(s32[96]{0:T(128)} %param.12) | copy-start | bytes 1156
  256.2 74.1 %all-gather.36.cloned.1.call-start = ((), (), s32[]{:S(2)}) async-start(), calls=%async_computation.8 | async-start | bytes 1769472 | tf_op jit(solution)/shard_map/all_gather | solution.py:48
  304.9 53.2 %all-gather.38.cloned.1.call-start = ((), (), s32[]{:S(2)}) async-start(), calls=%async_computation.9 | async-start | bytes 1769472 | tf_op jit(solution)/shard_map/all_gather | solution.py:21
  330.3 5.1 copy-start.4
  333.4 71.0 %all-gather.40.cloned.1.call-start = ((), (), s32[]{:S(2)}) async-start(), calls=%async_computation.10 | async-start | bytes 2506752 | tf_op jit(solution)/shard_map/all_gather | solution.py:27
  335.4 117.8 %all-gather.42.cloned.1.call-start = ((), (), s32[]{:S(2)}) async-start(), calls=%async_computation.11 | async-start | bytes 2506752 | tf_op jit(solution)/shard_map/all_gather | solution.py:27
  408.1 93.3 %all-gather.44.cloned.1.call-start = ((), (), s32[]{:S(2)}) async-start(), calls=%async_computation.12 | async-start | bytes 2506752 | tf_op jit(solution)/shard_map/all_gather | solution.py:27
  408.3 44.8 %copy-start.6 = (bf16[192,3072]{0,1:T(8,128)(2,1)S(1)}, bf16[192,3072]{0,1:T(8,128)(2,1)}, u32[]{:S(2)}) copy-start(bf16[192,3072]{0,1:T(8,128)(2,1)} %all-gather.38.cloned.1.call-done) | copy-start | bytes 3538948
  456.3 93.3 %all-gather.46.cloned.1.call-start = ((), (), s32[]{:S(2)}) async-start(), calls=%async_computation.13 | async-start | bytes 2506752 | tf_op jit(solution)/shard_map/all_gather | solution.py:27
  504.6 93.3 %all-gather.48.cloned.1.call-start = ((), (), s32[]{:S(2)}) async-start(), calls=%async_computation.14 | async-start | bytes 2506752 | tf_op jit(solution)/shard_map/all_gather | solution.py:27
  552.8 72.9 %all-gather.50.cloned.1.call-start = ((), (), s32[]{:S(2)}) async-start(), calls=%async_computation.15 | async-start | bytes 1327104 | tf_op jit(solution)/shard_map/all_gather | solution.py:21
  601.0 70.6 %all-gather.52.cloned.1.call-start = ((), (), s32[]{:S(2)}) async-start(), calls=%async_computation.16 | async-start | bytes 2506752 | tf_op jit(solution)/shard_map/all_gather | solution.py:27
  601.6 98.1 %all-gather.54.cloned.1.call-start = ((), (), s32[]{:S(2)}) async-start(), calls=%async_computation.17 | async-start | bytes 1327104 | tf_op jit(solution)/shard_map/all_gather | solution.py:21
  675.1 70.8 %all-gather.56.cloned.1.call-start = ((), (), s32[]{:S(2)}) async-start(), calls=%async_computation.18 | async-start | bytes 2506752 | tf_op jit(solution)/shard_map/all_gather | solution.py:27
Sparse Core Ops, SparseCore 0:
  9.0 27.0 all-gather.19
  38.3 43.9 all-gather.21
  84.0 24.4 all-gather.27
  110.5 43.9 all-gather.25
  156.0 24.4 all-gather.23
  182.6 43.9 all-gather.31
  228.2 24.4 all-gather.29
  256.4 43.9 all-gather.33
  305.0 25.2 all-gather.35
  333.6 24.4 all-gather.37
  360.3 44.1 all-gather.39
  408.2 44.8 all-gather.41
  456.4 44.8 all-gather.43
  504.7 44.8 all-gather.45
  552.9 44.8 all-gather.47
  601.1 24.4 all-gather.49
  627.7 43.9 all-gather.51
  675.2 24.4 all-gather.53
  701.9 43.9 all-gather.55
where the time goes:
time: 757 us; the launch traced here: 756 us
  waiting for transfers between devices  682 us (90%)
  matrix products  38.5 us (5%)
  local copies, waits for them, and re-layouts  16.9 us (2%)
  between operations  13.7 us (2%)
    all_gather x10, waiting for transfers between devices, panel_times(): lax.all_gather(matrix, 'row', axis=0, tiled=True)  448 us
    all_gather x7, waiting for transfers between devices, panel_rows(): return lax.all_gather(matrix, 'col', axis=1, tiled=True)  163 us
    all_gather x1, waiting for transfers between devices, reorder(): segment = lax.all_gather(generator, 'row', axis=0, tiled=True)  43.9 us
    dot_general x11, matrix products, panel_times(): jnp.dot(row_panel, lax.all_gather(matrix, 'row', axis=0, tiled=True), pre...  35.6 us
    all_gather x1, waiting for transfers between devices, reorder(): segment = lax.all_gather(by_rows, 'col', axis=1, tiled=True)  25.3 us
  transfers between devices with their start and end apart: 19, of which 19 were waited for; matrix products, arithmetic and copies ran while one was open for 3% of the time, Pallas kernels for 0%

commit v1 on v0

v1 whole, which is shorter than its diff:
```python
import jax
import jax.numpy as jnp
from jax import lax
from jax.experimental import pallas as pl
from jax.experimental.pallas import tpu as pltpu
from jax.sharding import PartitionSpec as P

MESH = pl.DeviceIdType.MESH
BLK = 32
TERMS = 6
RB = 6
CB = 12
TR = 192
TC = 384
N = 3072
NB = 96
SEMS = 320
BF = jnp.bfloat16
F32 = jnp.float32


def iota(shape, axis):
    return lax.broadcasted_iota(jnp.int32, shape, axis)


def mm(a, b):
    return jnp.dot(a, b, preferred_element_type=F32)


class Net:
    def __init__(self, send, recv):
        self.send, self.recv, self.used, self.copies = send, recv, 0, []

    def copy(self, src, dst, device):
        number = self.used
        self.used += 1
        made = pltpu.make_async_remote_copy(
            src, dst, self.send.at[number], self.recv.at[number], device_id=device, device_id_type=MESH
        )
        self.copies.append(made)
        return made

    def finish(self):
        for made in self.copies:
            made.wait_send()


class Ring:
    def __init__(self, net, k, after, before, piece):
        self.net = net
        p = lambda step, part: piece(lax.rem(k + step + 4, 4), part)
        c = lambda ref, device: net.copy(ref, ref, device)
        self.a0, self.b1 = c(p(0, 0), after), c(p(0, 1), before)
        self.a1, self.b0 = c(p(0, 1), after), c(p(0, 0), before)
        self.f0, self.f1 = c(p(-1, 0), after), c(p(1, 1), before)

    def start(self):
        for made in (self.a0, self.b1, self.a1, self.b0):
            made.start()

    def forward(self):
        self.a0.wait_recv()
        self.f0.start()
        self.b1.wait_recv()
        self.f1.start()

    def near(self):
        self.a1.wait_recv()
        self.b0.wait_recv()

    def far(self):
        self.f0.wait_recv()
        self.f1.wait_recv()


def body(
    fock, density, margin, fills, firsts, seconds, order_s, order_v, out,
    colp, cols_, colf, coly, colt, colz, blocks, rows, acc, masks, fl, xs, xr, send, recv, local,
):
    r, c = lax.axis_index("row"), lax.axis_index("col")
    y, z = r // 4, lax.rem(r, 4)
    x, core = c // 2, lax.rem(c, 2)
    net = Net(send, recv)

    def dev(yy, zz, xx, cc):
        return (lax.rem(yy + 4, 4) * 4 + lax.rem(zz + 4, 4), lax.rem(xx + 4, 4) * 2 + cc)

    yp, ym = dev(y + 1, z, x, core), dev(y - 1, z, x, core)
    zp, zm = dev(y, z + 1, x, core), dev(y, z - 1, x, core)
    xp, xm = dev(y, z, x + 1, core), dev(y, z, x - 1, core)
    sibling = (r, 2 * x + 1 - core)
    partners = [(2 * c + h, r // 2) for h in range(2)]
    itself = [jnp.logical_and(2 * c + h == r, r // 2 == c) for h in range(2)]

    barrier = pltpu.get_barrier_semaphore()
    others = [(r, lax.rem(c + k, 8)) for k in range(1, 8)]
    for device in others + [yp, ym, zp, zm]:
        pl.semaphore_signal(barrier, inc=1, device_id=device, device_id_type=MESH)
    for h in range(2):

        @pl.when(jnp.logical_not(itself[h]))
        def _():
            pl.semaphore_signal(barrier, inc=1, device_id=partners[h], device_id_type=MESH)

    pl.semaphore_wait(barrier, 13 - jnp.where(c == r // 2, 1, 0))

    class Columns:
        def __init__(self, buf):
            self.first = (
                Ring(net, z, zp, zm, lambda k, p: buf.at[y, k, pl.ds(48 * p, 48), :]),
                Ring(net, y, yp, ym, lambda k, p: buf.at[k, z, pl.ds(96 + 48 * p, 48), :]),
            )
            self.second = (
                Ring(net, y, yp, ym, lambda k, p: buf.at[k, :, pl.ds(48 * p, 48), :]),
                Ring(net, z, zp, zm, lambda k, p: buf.at[:, k, pl.ds(96 + 48 * p, 48), :]),
            )

        def s1(self):
            for ring in self.first:
                ring.start()

        def s1f(self):
            for ring in self.first:
                ring.forward()

        def s2(self):
            for ring in self.first:
                ring.near()
                ring.far()
                ring_number = self.first.index(ring)
                self.second[ring_number].start()

        def s2f(self):
            for ring in self.second:
                ring.forward()

        def done(self):
            for ring in self.second:
                ring.near()
                ring.far()

        def all(self):
            self.s1()
            self.s1f()
            self.s2()
            self.s2f()
            self.done()

    class Rows:
        def __init__(self, number):
            piece = lambda k, p: rows.at[number, pl.ds(96 * p, 96), pl.ds((2 * k + core) * TC, TC)]
            self.ring = Ring(net, x, xp, xm, piece)
            self.pairs = []
            for step in (0, -1, 1, 2):
                k = lax.rem(x + step + 4, 4)
                ref = rows.at[number, :, pl.ds((2 * k + core) * TC, TC)]
                self.pairs.append(net.copy(ref, ref, sibling))

        def start(self):
            self.ring.start()
            self.pairs[0].start()

        def forward(self):
            self.ring.forward()

        def near(self):
            self.ring.near()
            self.pairs[1].start()
            self.pairs[2].start()

        def far(self):
            self.ring.far()
            self.pairs[3].start()

        def done(self):
            for made in self.pairs:
                made.wait_recv()

        def all(self):
            self.start()
            self.forward()
            self.near()
            self.far()
            self.done()

    spread_rows = (iota((TR, RB), 0) // BLK == iota((TR, RB), 1)).astype(BF)
    spread_cols = (iota((CB, TC), 0) == iota((CB, TC), 1) // BLK).astype(BF)

    def expand(mask):
        wide = mm(mask.astype(F32).astype(BF), spread_cols).astype(BF)
        return mm(spread_rows, wide)

    def own(number):
        return rows.at[number, :, pl.ds(pl.multiple_of(c * TC, TC), TC)]

    def product(number, buf, start=None, sign=1.0):
        acc[...] = jnp.zeros_like(acc) if start is None else start

        @pl.loop(0, 4)
        def _(k):
            left = rows[number, :, pl.ds(pl.multiple_of(k * 768, 768), 768)]
            acc[...] += sign * mm(left, buf[k].reshape(768, TC))

    shift = (iota((CB, 128), 1) == c * CB + iota((CB, 128), 0)).astype(BF)
    pad8 = (iota((8, RB), 0) == iota((8, RB), 1)).astype(BF)
    for number in range(TERMS - 1):
        wide = mm(seconds[number].astype(F32).astype(BF), shift).astype(BF)
        fl[c, number] = mm(pad8, wide)

    get_p, get_s, get_f = Columns(colp), Columns(cols_), Columns(colf)
    row_f, row_s, row_g, row_h = Rows(0), Rows(1), Rows(2), Rows(3)

    colp[y, z] = (density[...].astype(F32) * expand(fills[1])).astype(BF)
    get_p.s1()
    masked = (fock[...].astype(F32) * expand(fills[0])).astype(BF)
    own(0)[...] = masked
    colf[y, z] = masked
    row_f.start()
    masked = (margin[...].astype(F32) * expand(fills[2])).astype(BF)
    own(1)[...] = masked
    cols_[y, z] = masked
    row_s.start()
    filters = []
    for device in others:
        made = net.copy(fl.at[c], fl.at[c], device)
        made.start()
        filters.append(made)
    get_p.s1f()
    row_f.forward()
    get_p.s2()
    row_f.near()
    for number in range(3):
        masks[number] = expand(firsts[number]).astype(BF)
    row_s.forward()
    row_f.far()
    get_p.s2f()
    get_s.s1()
    row_s.near()
    row_s.far()
    row_f.done()
    get_p.done()
    get_s.s1f()
    product(0, colp)
    own(2)[...] = (acc[...] * masks[0].astype(F32)).astype(BF)
    row_g.start()
    row_s.done()
    get_s.s2()
    product(1, colp)
    own(3)[...] = (acc[...] * masks[1].astype(F32)).astype(BF)
    row_h.start()
    row_g.forward()
    row_g.near()
    row_h.forward()
    get_s.s2f()
    get_f.s1()
    row_g.far()
    row_h.near()
    row_h.far()
    row_g.done()
    row_h.done()
    for made in filters:
        made.wait_recv()

    total = fl[0]
    for number in range(1, 8):
        total = total + fl[number]
    spread8 = (iota((TR, 8), 0) // BLK == iota((TR, 8), 1)).astype(BF)
    place = (order_v[...] == c * CB + iota((128, TC), 1) // BLK).astype(BF)
    for number in range(TERMS - 1):
        wide = mm(total[number].astype(BF), place).astype(BF)
        masks[3 + number] = mm(spread8, wide).astype(BF)
    mine = (iota((8, 128), 1) == r * RB + iota((8, 128), 0)).astype(BF)
    wide = mm(mine, place).astype(BF)
    same = lax.rem(iota((TR, TC), 0), BLK) == lax.rem(iota((TR, TC), 1), BLK)
    masks[8] = jnp.where(same, mm(spread8, wide), 0.0).astype(BF)
    masks[9] = expand(seconds[TERMS - 1]).astype(BF)
    masks[10] = expand(seconds[TERMS]).astype(BF)

    get_s.done()
    get_f.s1f()
    product(2, cols_)
    get_f.s2()
    get_f.s2f()
    get_f.done()

    @pl.loop(0, 4)
    def _(k):
        left = rows[3, :, pl.ds(pl.multiple_of(k * 768, 768), 768)]
        acc[...] -= mm(left, colf[k].reshape(768, TC))

    def exchange(number, tile):
        turned = tile.T.astype(BF)
        made = []
        for h in range(2):
            xs[number, h] = turned[TR * h : TR * (h + 1), :]
        for h in range(2):
            copy = pltpu.make_async_remote_copy(
                xs.at[number, h], xr.at[number, lax.rem(r, 2)], send.at[SEMS - 4 + 2 * number + h],
                recv.at[SEMS - 4 + 2 * number + lax.rem(r, 2)], device_id=partners[h], device_id_type=MESH,
            )
            here = pltpu.make_async_copy(xs.at[number, h], xr.at[number, h], local.at[number])
            made.append((copy, here))

            @pl.when(itself[h])
            def _():
                here.start()

            @pl.when(jnp.logical_not(itself[h]))
            def _():
                copy.start()

        value = None
        for h in range(2):
            copy, here = made[h]
            arrival = pltpu.make_async_remote_copy(
                xs.at[number, h], xr.at[number, h], send.at[SEMS - 4 + 2 * number + h],
                recv.at[SEMS - 4 + 2 * number + h], device_id=partners[h], device_id_type=MESH,
            )

            @pl.when(itself[h])
            def _():
                here.wait()

            @pl.when(jnp.logical_not(itself[h]))
            def _():
                arrival.wait_recv()
                copy.wait_send()

            lane = (iota((TR, TC), 0) + TR * h == iota((TR, TC), 1)).astype(BF)
            part = mm(xr[number, h], lane)
            value = part if value is None else value + part
        return value

    tile = (acc[...] * masks[2].astype(F32)).astype(BF)
    turned = exchange(0, tile.astype(F32))
    coly[y, z] = (turned * 0.25).astype(BF)
    Columns(coly).all()

    def by_blocks(buf):
        @pl.loop(0, 4)
        def _(k):
            blocks[pl.ds(24 * k, 24)] = buf[k].reshape(24, BLK, TC)

    by_blocks(coly)
    for b in range(RB):
        part = blocks[order_s[r * RB + b]].astype(F32)
        own(4)[pl.ds(BLK * b, BLK), :] = (masks[8, pl.ds(BLK * b, BLK), :].astype(F32) + part / 6.0).astype(BF)
    for number in range(TERMS - 1):
        Rows(4 + number).all()
        product(4 + number, coly)
        filtered = acc[...] * masks[3 + number].astype(F32)
        value = masks[8].astype(F32) + filtered / float(TERMS - 1 - number)
        if number < TERMS - 2:
            own(5 + number)[...] = value.astype(BF)

    turned = exchange(1, value.astype(BF).astype(F32))
    colt[y, z] = turned.astype(BF)
    Columns(colt).all()
    by_blocks(colt)
    for b in range(RB):
        own(9)[pl.ds(BLK * b, BLK), :] = blocks[order_s[r * RB + b]]
    row_t = Rows(9)
    row_t.start()
    row_t.forward()
    row_t.near()
    row_t.far()
    row_t.done()
    acc[...] = jnp.zeros_like(acc)

    @pl.loop(0, 4)
    def _(k):
        left = rows[9, :, pl.ds(pl.multiple_of(k * 768, 768), 768)]
        right = jnp.concatenate([blocks[order_s[24 * k + b]] for b in range(24)], axis=0)
        acc[...] += mm(left, right)

    value = (acc[...] * masks[9].astype(F32)).astype(BF)
    own(10)[...] = value
    colz[y, z] = value
    row_z, get_z = Rows(10), Columns(colz)
    get_z.s1()
    row_z.start()
    get_z.s1f()
    row_z.forward()
    get_z.s2()
    row_z.near()
    row_z.far()
    row_z.done()
    get_z.s2f()
    get_z.done()
    product(10, colz)
    out[...] = (acc[...] * masks[10].astype(F32)).astype(BF)
    net.finish()
    assert net.used <= SEMS - 4


def on_device(fock, density, margin, fills, firsts, owner_order, seconds):
    vmem = pl.BlockSpec(memory_space=pltpu.VMEM)
    order_v = jnp.pad(owner_order, (0, 128 - owner_order.shape[0]), constant_values=-1)[:, None]
    panel = pltpu.VMEM((4, 4, TR, TC), BF)
    return pl.pallas_call(
        body,
        out_shape=jax.ShapeDtypeStruct((TR, TC), BF),
        in_specs=[vmem] * 6 + [pl.BlockSpec(memory_space=pltpu.SMEM), vmem],
        out_specs=vmem,
        scratch_shapes=[panel] * 6
        + [
            pltpu.VMEM((NB, BLK, TC), BF),
            pltpu.VMEM((11, TR, N), BF),
            pltpu.VMEM((TR, TC), F32),
            pltpu.VMEM((11, TR, TC), BF),
            pltpu.VMEM((8, TERMS - 1, 8, 128), F32),
            pltpu.VMEM((2, 2, TR, TR), BF),
            pltpu.VMEM((2, 2, TR, TR), BF),
            pltpu.SemaphoreType.DMA((SEMS,)),
            pltpu.SemaphoreType.DMA((SEMS,)),
            pltpu.SemaphoreType.DMA((2,)),
        ],
        compiler_params=pltpu.CompilerParams(
            collective_id=0, has_side_effects=True, vmem_limit_bytes=60 * 1024 * 1024
        ),
    )(fock, density, margin, fills, firsts, seconds, owner_order, order_v)


def solution(mesh):
    return jax.shard_map(
        on_device,
        mesh=mesh,
        in_specs=(
            P("row", "col"),
            P("row", "col"),
            P("row", "col"),
            P(None, "row", "col"),
            P(None, "row", "col"),
            P(),
            P(None, "row", "col"),
        ),
        out_specs=P("row", "col"),
        check_vma=False,
    )
```

time: 757 us -> 215 us (0.28)
  waiting for transfers between devices: 682 us -> 0 us
  Pallas kernels: 0 us -> 210 us
  matrix products: 38.5 us -> 0 us
  between operations: 13.7 us -> 0.01 us
  local copies, waits for them, and re-layouts: 16.9 us -> 4.33 us
    all_gather x19 -> x0, waiting for transfers between devices: 680 us -> none  [the longest x10 448 us: panel_times(): lax.all_gather(matrix, 'row', axis=0, tiled=True)]
    pallas_call x0 -> x1, Pallas kernels: none -> 210 us  [on_device(): pl.pallas_call(body, out_shape=jax.ShapeDtypeStruct((TR, TC), BF), in_spe...]
    dot_general x13 -> x0, matrix products: 38.5 us -> none  [the longest x11 35.6 us: panel_times(): jnp.dot(row_panel, lax.all_gather(matrix, 'row', axis=0, tiled=True), pre...]
    mul x27 -> x0, local copies, waits for them, and re-layouts: 11.5 us -> none  [the longest x26 10.8 us: expand(): values.reshape(row_blocks, BLK, column_blocks, BLK)]
  transfers between devices with their start and end apart: 19 -> 0, of which waited for: 19 -> 0; matrix products, arithmetic and copies ran while one was open for 3% -> 0% of each run, Pallas kernels for 0% -> 0%
where the time goes in v1:
time: 215 us; the launch traced here: 214 us
  Pallas kernels  210 us (98%)
  local copies, waits for them, and re-layouts  4.33 us (2%)
    pallas_call x1, Pallas kernels, on_device(): pl.pallas_call(body, out_shape=jax.ShapeDtypeStruct((TR, TC), BF), in_spe...  210 us

profile of v1, /device:TPU:1, one launch (start us, length us, event | category | flops | bytes accessed | tf_op | source)
XLA Modules:
  0.0 214.4 jit_solution(17885054982743199969)
XLA Ops:
  0.0 0.7 pad_bitcast_fusion
  0.7 1.3 copy.8.seconds
  2.0 0.7 copy.9.order_v
  2.7 210.1 %shard_map.73 = bf16[192,384]{1,0:T(8,128)(2,1)} custom-call(bf16[192,384]{1,0:T(8,128)(2,1)} %fock.1, bf16[192,384]{1,0:T(8,128)(2,1)} %density.1, bf16[192,384]{1,0:T(8,128)(2,1)} %margin.1, s32[3,6,12]{2,1,0:T(8,128)} %fills.1, s32[3,6,12]{2,1,0:T(8,128)} %firsts.1, s32[7,6,12]{2,1,0:T(8,128)} %copy.8.seconds, s32[96]{0:T(128)} %order_s.1, ...), custom_call_target="tpu_custom_call" | custom-call | tf_op jit(solution)/shard_map/pallas_call | solution.py:400
  212.8 1.6 copy.11

commit v2 on v0

v2 whole, which is shorter than its diff:
```python
import jax
import jax.numpy as jnp
from jax import lax
from jax.experimental import pallas as pl
from jax.experimental.pallas import tpu as pltpu
from jax.sharding import PartitionSpec as P

MESH = pl.DeviceIdType.MESH
BLK = 32
TERMS = 6
RB = 6
CB = 12
TR = 192
TC = 384
N = 3072
NB = 96
SEMS = 336
BF = jnp.bfloat16
F32 = jnp.float32


def iota(shape, axis):
    return lax.broadcasted_iota(jnp.int32, shape, axis)


def mm(a, b):
    return jnp.dot(a, b, preferred_element_type=F32)


class Net:
    def __init__(self, sems, units):
        self.sems, self.units, self.used, self.groups = sems, units, 0, []

    def sem(self):
        self.used += 1
        return self.sems.at[self.used - 1]

    def group(self):
        made = [self.sem(), 0]
        return made

    def senders(self):
        made = self.group()
        self.groups.append(made)
        return made

    def copy(self, ref, device, sent, size, got=None, target=None):
        if got is None:
            got = self.sem()
        elif isinstance(got, list):
            got[1] += size
            got = got[0]
        sent[1] += size
        return pltpu.make_async_remote_copy(
            ref, ref if target is None else target, sent[0], got, device_id=device, device_id_type=MESH
        )

    def wait(self, group):
        ref = self.units.at[pl.ds(0, group[1])]
        pltpu.make_async_copy(ref, ref, group[0]).wait()

    def finish(self):
        for made in self.groups:
            self.wait(made)


class Ring:
    def __init__(self, net, k, nexts, piece, sizes, sent, near=None, far=None):
        after, before = nexts
        p = lambda step, part: piece(lax.rem(k + step + 4, 4), part)
        c = lambda step, part, device, got=None: net.copy(p(step, part), device, sent, sizes[part], got)
        self.a0, self.b1 = c(0, 0, after), c(0, 1, before)
        self.a1, self.b0 = c(0, 1, after, near), c(0, 0, before, near)
        self.f0, self.f1 = c(-1, 0, after, far), c(1, 1, before, far)

    def start(self):
        for made in (self.a0, self.b1, self.a1, self.b0):
            made.start()

    def forward(self):
        self.a0.wait_recv()
        self.f0.start()
        self.b1.wait_recv()
        self.f1.start()

    def near(self):
        self.a1.wait_recv()
        self.b0.wait_recv()

    def far(self):
        self.f0.wait_recv()
        self.f1.wait_recv()


class Plane:
    def __init__(self, net, k1, next1, k2, next2, piece_a, piece_b, sizes_a, sizes_b):
        self.net = net
        sends = [net.senders(), net.senders()]
        turn = lambda k, s: lax.rem(k + s + 4, 4)
        steps = (0, -1, 1, 2)
        self.ends = []

        def second(k, nexts, piece, sizes, sent):
            rings = []
            for s in steps:
                end = net.group()
                self.ends.append(end)
                rings.append(Ring(net, k, nexts, piece(s), sizes, sent, end, end))
            return rings

        self.a1 = Ring(net, k1, next1, lambda k, p: piece_a(k, k2, p), sizes_a, sends[0])
        self.a2 = second(k2, next2, lambda s: lambda k, p: piece_a(turn(k1, s), k, p), sizes_a, sends[0])
        self.b1 = Ring(net, k2, next2, lambda k, p: piece_b(k1, k, p), sizes_b, sends[1])
        self.b2 = second(k1, next1, lambda s: lambda k, p: piece_b(k, turn(k2, s), p), sizes_b, sends[1])

    def s1(self):
        self.a1.start()
        self.b1.start()
        self.a2[0].start()
        self.b2[0].start()

    def s2(self):
        self.a1.forward()
        self.b1.forward()
        for first, rings in ((self.a1, self.a2), (self.b1, self.b2)):
            first.near()
            rings[1].start()
            rings[2].start()

    def s3(self):
        self.a2[0].forward()
        self.b2[0].forward()
        for first, rings in ((self.a1, self.a2), (self.b1, self.b2)):
            first.far()
            rings[3].start()

    def s4(self):
        for number in (1, 2, 3):
            self.a2[number].forward()
            self.b2[number].forward()

    def end(self, number):
        self.net.wait(self.ends[number])

    def done(self):
        for number in range(8):
            self.end(number)


def body(
    fock, density, margin, fills, firsts, seconds, order, out,
    colp, cols_, colf, colt, colz, panel, series, units, rows, acc, masks, filters, place, turned, arrived, sems,
):
    r, c = lax.axis_index("row"), lax.axis_index("col")
    y, z = r // 4, lax.rem(r, 4)
    x, core = c // 2, lax.rem(c, 2)
    net = Net(sems, units)

    def dev(yy, zz, xx):
        return (lax.rem(yy + 4, 4) * 4 + lax.rem(zz + 4, 4), lax.rem(xx + 4, 4) * 2 + core)

    next_y = (dev(y + 1, z, x), dev(y - 1, z, x))
    next_z = (dev(y, z + 1, x), dev(y, z - 1, x))
    next_x = (dev(y, z, x + 1), dev(y, z, x - 1))
    across = dev(y, z + 2, x)
    sibling = (r, 2 * x + 1 - core)

    barrier = pltpu.get_barrier_semaphore()
    for device in next_y + next_z + next_x + (across, sibling):
        pl.semaphore_signal(barrier, inc=1, device_id=device, device_id_type=MESH)
    pl.semaphore_wait(barrier, 8)

    def columns(buf, extra=0):
        parts = ((0, 48), (48, 48)), ((96, 48), (144, 48 + extra))
        piece = lambda cut: lambda k1, k2, p: buf.at[k2, k1, pl.ds(*cut[p]), :]
        sizes = [[size // 16 for _, size in cut] for cut in parts]
        return Plane(net, z, next_z, y, next_y, piece(parts[0]), piece(parts[1]), *sizes)

    class Rows:
        def __init__(self, number):
            sent = net.senders()
            piece = lambda k, p: rows.at[number, pl.ds(96 * p, 96), pl.ds((2 * k + core) * TC, TC)]
            self.ring = Ring(net, x, next_x, piece, (6, 6), sent)
            self.pairs, self.end = [], net.group()
            for step in (0, -1, 1, 2):
                k = lax.rem(x + step + 4, 4)
                ref = rows.at[number, :, pl.ds((2 * k + core) * TC, TC)]
                self.pairs.append(net.copy(ref, sibling, sent, 12, self.end))

        def start(self):
            self.ring.start()
            self.pairs[0].start()

        def forward(self):
            self.ring.forward()

        def near(self):
            self.ring.near()
            self.pairs[1].start()
            self.pairs[2].start()

        def far(self):
            self.ring.far()
            self.pairs[3].start()

        def done(self):
            net.wait(self.end)

    spread_rows = (iota((TR, RB), 0) // BLK == iota((TR, RB), 1)).astype(BF)
    spread_cols = (iota((CB, TC), 0) == iota((CB, TC), 1) // BLK).astype(BF)

    def expand(mask):
        wide = mm(mask.astype(F32).astype(BF), spread_cols).astype(BF)
        return mm(spread_rows, wide)

    def own(number):
        return rows.at[number, :, pl.ds(pl.multiple_of(c * TC, TC), TC)]

    def product(number, buf, sign=0):
        if not sign:
            acc[...] = jnp.zeros_like(acc)

        @pl.loop(0, 4)
        def _(k):
            left = rows[number, :, pl.ds(pl.multiple_of(k * 768, 768), 768)]
            right = buf[k, :, pl.ds(0, TR), :].reshape(768, TC)
            if sign:
                acc[...] -= mm(left, right)
            else:
                acc[...] += mm(left, right)

    colp[y, z] = (density[...].astype(F32) * expand(fills[1])).astype(BF)
    get_p = columns(colp)
    get_p.s1()
    row_f, row_s, row_g, row_h = [Rows(number) for number in range(4)]
    masked = (fock[...].astype(F32) * expand(fills[0])).astype(BF)
    own(0)[...] = masked
    row_f.start()
    colf[y, z, pl.ds(0, TR), :] = masked
    masked = (margin[...].astype(F32) * expand(fills[2])).astype(BF)
    own(1)[...] = masked
    row_s.start()
    cols_[y, z] = masked
    get_s, get_f = columns(cols_), columns(colf, 16)
    get_p.s2()
    row_f.forward()
    packed = jnp.zeros((16, TC), F32)
    pad16 = (iota((16, RB), 0) == iota((16, RB), 1)).astype(BF)
    for number in range(TERMS - 1):
        shift = (iota((CB, TC), 1) == CB * number + iota((CB, TC), 0)).astype(BF)
        packed += mm(mm(pad16, seconds[number].astype(F32).astype(BF)).astype(BF), shift)
    colf[y, z, pl.ds(TR, 16), :] = packed.astype(BF)
    get_p.s3()
    row_f.near()
    row_s.forward()
    for number in range(3):
        masks[number] = expand(firsts[number]).astype(BF)
    get_p.s4()
    get_s.s1()
    row_f.far()
    row_s.near()
    row_s.far()
    row_f.done()
    get_p.done()
    get_s.s2()
    product(0, colp)
    own(2)[...] = (acc[...] * masks[0].astype(F32)).astype(BF)
    row_g.start()
    row_s.done()
    get_s.s3()
    product(1, colp)
    own(3)[...] = (acc[...] * masks[1].astype(F32)).astype(BF)
    row_h.start()
    get_s.s4()
    get_f.s1()
    row_g.forward()
    row_g.near()
    row_h.forward()
    row_g.far()
    row_h.near()
    row_h.far()
    row_g.done()
    row_h.done()

    column_block = 24 * y + iota((1, 768), 1) // BLK
    place[...] = jnp.zeros_like(place)

    @pl.loop(0, 16)
    def _(k):
        for i in range(RB):
            place[pl.ds(16 * k + i, 1), :] = (column_block == order[RB * k + i]).astype(F32)

    base = CB * c + 3 * z
    same = lax.rem(iota((BLK, 768), 0), BLK) == lax.rem(iota((BLK, 768), 1), BLK)
    for i in range(3):
        mine = order[base + i]
        for k in range(4):
            hit = jnp.logical_and(same, iota((BLK, 768), 1) // BLK + 24 * k == mine)
            series[0, k, pl.ds(BLK * i, BLK), :] = hit.astype(F32).astype(BF)
        hit = jnp.logical_and(same, iota((BLK, 768), 1) // BLK + 24 * y == mine)
        filters[5, pl.ds(BLK * i, BLK), :] = hit.astype(F32).astype(BF)
    masks[3] = expand(seconds[TERMS - 1]).astype(BF)
    masks[4] = expand(seconds[TERMS]).astype(BF)
    get_s.done()
    get_f.s2()
    product(2, cols_)
    get_f.s3()
    get_f.s4()
    get_f.done()
    product(3, colf, -1)

    tile = (acc[...] * masks[2].astype(F32)).astype(BF)
    panel[x, core, z] = (tile.astype(F32) * 0.25).astype(BF)
    cut = lambda base: lambda k1, k2, p: panel.at[k2, core, k1, pl.ds(base + 48 * p, 48), :]
    get_x = Plane(net, z, next_z, x, next_x, cut(0), cut(96), (3, 3), (3, 3))
    get_x.s1()
    sent, pairs, end = net.senders(), [], net.group()
    for s in (0, -1, 1, 2):
        ref = panel.at[:, core, lax.rem(z + s + 4, 4), pl.ds(0, 96), :]
        pairs.append(net.copy(ref, sibling, sent, 24, end))
    for s in (0, -1, 1, 2):
        ref = panel.at[lax.rem(x + s + 4, 4), core, :, pl.ds(96, 96), :]
        pairs.append(net.copy(ref, sibling, sent, 24, end))
    get_x.s2()
    get_x.s3()
    get_x.s4()
    spread = (iota((16 * 24, 96), 0) - 3 * z).astype(jnp.int32)
    known = colf[:, :, pl.ds(TR, 16), :].reshape(256, TC)
    for number in range(TERMS - 1):
        pick = (spread == CB * number + iota((16 * 24, 96), 1) // BLK).astype(BF)
        wide = mm(known, pick).astype(BF)
        filters[number] = lax.dot_general(
            wide, place[...].astype(BF), (((0,), (0,)), ((), ())), preferred_element_type=F32
        ).astype(BF)
    for number in (0, 4, 1, 2, 5, 6, 3, 7):
        get_x.end(number)
        pairs[number].start()
    net.wait(end)

    def piece_times(step, k, half):
        left = series[step, k, pl.ds(48 * half, 48), :]
        total = None
        for h in range(2):
            part = lax.dot_general(
                left[:, TC * h : TC * (h + 1)], panel[k, h].reshape(768, TC),
                (((1,), (1,)), ((), ())), preferred_element_type=F32,
            )
            total = part if total is None else total + part
        return total

    def filtered(step, half, total):
        cut = pl.ds(48 * half, 48)
        eye = filters[5, cut, :].astype(F32)
        if step == 0:
            return eye + total / float(TERMS)
        return eye + total * filters[step - 1, cut, :].astype(F32) / float(TERMS - step)

    class Turn:
        def __init__(self, step, half):
            self.step, self.half = step, half
            self.near, self.far = net.group(), net.group()
            piece = lambda k, p: series.at[step, k, pl.ds(48 * half, 48), pl.ds(TC * p, TC)]
            self.ring = Ring(net, y, next_y, piece, (3, 3), net.senders(), self.near, self.far)

        def start(self):
            self.ring.start()
            sums[self.half] = piece_times(self.step, y, self.half)

        def forward(self):
            self.ring.forward()

        def finish(self):
            net.wait(self.near)
            total = sums[self.half]
            for s in (-1, 1):
                total += piece_times(self.step, lax.rem(y + s + 4, 4), self.half)
            net.wait(self.far)
            total += piece_times(self.step, lax.rem(y + 2, 4), self.half)
            return filtered(self.step, self.half, total)

    sums = {}

    def put(step, half, value):
        series[step, y, pl.ds(48 * half, 48), :] = value.astype(BF)

    turns = [[Turn(step, half) for half in range(2)] for step in range(1, TERMS)]
    for half in range(2):
        total = piece_times(0, 0, half)
        for k in range(1, 4):
            total += piece_times(0, k, half)
        put(1, half, filtered(0, half, total))
        turns[0][half].start()
    last = []
    for step in range(1, TERMS):
        for half in range(2):
            turns[step - 1][half].forward()
        for half in range(2):
            value = turns[step - 1][half].finish()
            if step < TERMS - 1:
                put(step + 1, half, value)
                turns[step][half].start()
            else:
                last.append(value)

    flat = jnp.concatenate(last, axis=0).T.astype(BF)
    for k in range(4):
        turned[k] = flat[TR * k : TR * (k + 1), :]
    made = []
    for s, device in ((1, next_z[0]), (-1, next_z[1]), (2, across)):
        made.append(net.copy(turned.at[lax.rem(z + s + 4, 4)], device, [net.sem(), 0], 0, None, arrived.at[z]))
    for copy in made:
        copy.start()
    arrived[z] = turned[z]
    for copy in made:
        copy.wait()
    value = jnp.zeros((TR, TC), F32)
    for k in range(4):
        lane = (iota((96, TC), 0) + 96 * k == iota((96, TC), 1)).astype(BF)
        value += mm(arrived[k], lane)
    colt[y, z] = value.astype(BF)
    get_t = columns(colt)
    get_t.s1()
    get_t.s2()
    get_t.s3()
    get_t.s4()
    get_t.done()

    @pl.loop(0, 4)
    def _(k):
        units[pl.ds(48 * k, 48)] = colt[k].reshape(48, 16, TC)

    for b in range(RB):
        for h in range(2):
            own(4)[pl.ds(BLK * b + 16 * h, 16), :] = units[2 * order[r * RB + b] + h]
    row_t = Rows(4)
    row_t.start()
    row_t.forward()
    row_t.near()
    row_t.far()
    row_t.done()
    acc[...] = jnp.zeros_like(acc)

    @pl.loop(0, 4)
    def _(k):
        left = rows[4, :, pl.ds(pl.multiple_of(k * 768, 768), 768)]
        right = jnp.concatenate([units[2 * order[24 * k + b] + h] for b in range(24) for h in range(2)], axis=0)
        acc[...] += mm(left, right)

    value = (acc[...] * masks[3].astype(F32)).astype(BF)
    own(5)[...] = value
    colz[y, z] = value
    row_z, get_z = Rows(5), columns(colz)
    get_z.s1()
    row_z.start()
    get_z.s2()
    row_z.forward()
    get_z.s3()
    row_z.near()
    get_z.s4()
    row_z.far()
    row_z.done()
    get_z.done()
    product(5, colz)
    out[...] = (acc[...] * masks[4].astype(F32)).astype(BF)
    net.finish()
    assert net.used <= SEMS, net.used


def on_device(fock, density, margin, fills, firsts, owner_order, seconds):
    vmem = pl.BlockSpec(memory_space=pltpu.VMEM)
    panel = pltpu.VMEM((4, 4, TR, TC), BF)
    return pl.pallas_call(
        body,
        out_shape=jax.ShapeDtypeStruct((TR, TC), BF),
        in_specs=[vmem] * 6 + [pl.BlockSpec(memory_space=pltpu.SMEM)],
        out_specs=vmem,
        scratch_shapes=[
            panel,
            panel,
            pltpu.VMEM((4, 4, TR + 16, TC), BF),
            panel,
            panel,
            pltpu.VMEM((4, 2, 4, TR, TC), BF),
            pltpu.VMEM((TERMS, 4, 96, 768), BF),
            pltpu.VMEM((192, 16, TC), BF),
            pltpu.VMEM((6, TR, N), BF),
            pltpu.VMEM((TR, TC), F32),
            pltpu.VMEM((5, TR, TC), BF),
            pltpu.VMEM((6, 96, 768), BF),
            pltpu.VMEM((256, 768), F32),
            pltpu.VMEM((4, TR, 96), BF),
            pltpu.VMEM((4, TR, 96), BF),
            pltpu.SemaphoreType.DMA((SEMS,)),
        ],
        compiler_params=pltpu.CompilerParams(
            collective_id=0, has_side_effects=True, vmem_limit_bytes=60 * 1024 * 1024
        ),
    )(fock, density, margin, fills, firsts, seconds, owner_order)


def solution(mesh):
    return jax.shard_map(
        on_device,
        mesh=mesh,
        in_specs=(
            P("row", "col"),
            P("row", "col"),
            P("row", "col"),
            P(None, "row", "col"),
            P(None, "row", "col"),
            P(),
            P(None, "row", "col"),
        ),
        out_specs=P("row", "col"),
        check_vma=False,
    )
```

time: 757 us -> 170 us (0.22)
  waiting for transfers between devices: 682 us -> 0 us
  Pallas kernels: 0 us -> 167 us
  matrix products: 38.5 us -> 0 us
  local copies, waits for them, and re-layouts: 16.9 us -> 2.94 us
  between operations: 13.7 us -> 0.01 us
    all_gather x19 -> x0, waiting for transfers between devices: 680 us -> none  [the longest x10 448 us: panel_times(): lax.all_gather(matrix, 'row', axis=0, tiled=True)]
    pallas_call x0 -> x1, Pallas kernels: none -> 167 us  [on_device(): pl.pallas_call(body, out_shape=jax.ShapeDtypeStruct((TR, TC), BF), in_spe...]
    dot_general x13 -> x0, matrix products: 38.5 us -> none  [the longest x11 35.6 us: panel_times(): jnp.dot(row_panel, lax.all_gather(matrix, 'row', axis=0, tiled=True), pre...]
    mul x27 -> x0, local copies, waits for them, and re-layouts: 11.5 us -> none  [the longest x26 10.8 us: expand(): values.reshape(row_blocks, BLK, column_blocks, BLK)]
  transfers between devices with their start and end apart: 19 -> 0, of which waited for: 19 -> 0; matrix products, arithmetic and copies ran while one was open for 3% -> 0% of each run, Pallas kernels for 0% -> 0%
where the time goes in v2:
time: 170 us; the launch traced here: 169 us
  Pallas kernels  167 us (98%)
  local copies, waits for them, and re-layouts  2.94 us (2%)
    pallas_call x1, Pallas kernels, on_device(): pl.pallas_call(body, out_shape=jax.ShapeDtypeStruct((TR, TC), BF), in_spe...  167 us

profile of v2, /device:TPU:1, one launch (start us, length us, event | category | flops | bytes accessed | tf_op | source)
XLA Modules:
  0.0 169.5 jit_solution(17570803479343816720)
XLA Ops:
  0.0 1.4 copy.8.seconds
  1.4 166.5 %shard_map.73 = bf16[192,384]{1,0:T(8,128)(2,1)} custom-call(bf16[192,384]{1,0:T(8,128)(2,1)} %fock.1, bf16[192,384]{1,0:T(8,128)(2,1)} %density.1, bf16[192,384]{1,0:T(8,128)(2,1)} %margin.1, s32[3,6,12]{2,1,0:T(8,128)} %fills.1, s32[3,6,12]{2,1,0:T(8,128)} %firsts.1, s32[7,6,12]{2,1,0:T(8,128)} %copy.8.seconds, s32[96]{0:T(128)} %order.1), custom_call_target="tpu_custom_call" | custom-call | tf_op jit(solution)/shard_map/pallas_call | solution.py:472
  167.9 1.6 copy.10

commit v3 on v2

--- a/solution.py
+++ b/solution.py
@@ -14,7 +14,7 @@
 TC = 384
 N = 3072
 NB = 96
-SEMS = 336
+SEMS = 154
 BF = jnp.bfloat16
 F32 = jnp.float32
 
@@ -30,10 +30,22 @@
 class Net:
     def __init__(self, sems, units):
         self.sems, self.units, self.used, self.groups = sems, units, 0, []
+        self.spare, self.taken = [], []
 
     def sem(self):
-        self.used += 1
-        return self.sems.at[self.used - 1]
+        if self.spare:
+            made = self.spare.pop(0)
+        else:
+            made = self.used
+            self.used += 1
+        self.taken.append(made)
+        return self.sems.at[made]
+
+    def release(self, owner):
+        for sent in owner.sends:
+            self.wait(sent)
+            self.groups = [made for made in self.groups if made is not sent]
+        self.spare.extend(owner.held)
 
     def group(self):
         made = [self.sem(), 0]
@@ -95,6 +107,7 @@
 class Plane:
     def __init__(self, net, k1, next1, k2, next2, piece_a, piece_b, sizes_a, sizes_b):
         self.net = net
+        net.taken = []
         sends = [net.senders(), net.senders()]
         turn = lambda k, s: lax.rem(k + s + 4, 4)
         steps = (0, -1, 1, 2)
@@ -112,6 +125,7 @@
         self.a2 = second(k2, next2, lambda s: lambda k, p: piece_a(turn(k1, s), k, p), sizes_a, sends[0])
         self.b1 = Ring(net, k2, next2, lambda k, p: piece_b(k1, k, p), sizes_b, sends[1])
         self.b2 = second(k1, next1, lambda s: lambda k, p: piece_b(k, turn(k2, s), p), sizes_b, sends[1])
+        self.sends, self.held = sends, net.taken
 
     def s1(self):
         self.a1.start()
@@ -178,33 +192,43 @@
 
     class Rows:
         def __init__(self, number):
+            net.taken = []
             sent = net.senders()
             piece = lambda k, p: rows.at[number, pl.ds(96 * p, 96), pl.ds((2 * k + core) * TC, TC)]
             self.ring = Ring(net, x, next_x, piece, (6, 6), sent)
-            self.pairs, self.end = [], net.group()
-            for step in (0, -1, 1, 2):
-                k = lax.rem(x + step + 4, 4)
-                ref = rows.at[number, :, pl.ds((2 * k + core) * TC, TC)]
-                self.pairs.append(net.copy(ref, sibling, sent, 12, self.end))
+            self.ends = [net.group(), net.group(), net.group()]
+            turn = lambda s: lax.rem(x + s + 4, 4)
+            give = lambda s, p, end: net.copy(piece(turn(s), p), sibling, sent, 6, self.ends[end])
+            self.own = (give(0, 0, 0), give(0, 1, 0))
+            self.nears = (give(-1, 0, 1), give(1, 1, 1), give(-1, 1, 1), give(1, 0, 1))
+            self.fars = (give(2, 0, 2), give(2, 1, 2))
+            self.sends, self.held = [sent], net.taken
 
         def start(self):
             self.ring.start()
-            self.pairs[0].start()
+            for made in self.own:
+                made.start()
 
         def forward(self):
-            self.ring.forward()
+            ring = self.ring
+            for got, further, give in ((ring.a0, ring.f0, 0), (ring.b1, ring.f1, 1)):
+                got.wait_recv()
+                further.start()
+                self.nears[give].start()
 
         def near(self):
-            self.ring.near()
-            self.pairs[1].start()
-            self.pairs[2].start()
+            for got, give in ((self.ring.a1, 2), (self.ring.b0, 3)):
+                got.wait_recv()
+                self.nears[give].start()
 
         def far(self):
-            self.ring.far()
-            self.pairs[3].start()
+            for got, give in ((self.ring.f0, 0), (self.ring.f1, 1)):
+                got.wait_recv()
+                self.fars[give].start()
 
         def done(self):
-            net.wait(self.end)
+            for end in self.ends:
+                net.wait(end)
 
     spread_rows = (iota((TR, RB), 0) // BLK == iota((TR, RB), 1)).astype(BF)
     spread_cols = (iota((CB, TC), 0) == iota((CB, TC), 1) // BLK).astype(BF)
@@ -236,20 +260,20 @@
     masked = (fock[...].astype(F32) * expand(fills[0])).astype(BF)
     own(0)[...] = masked
     row_f.start()
-    colf[y, z, pl.ds(0, TR), :] = masked
+    colf[y, z] = masked
     masked = (margin[...].astype(F32) * expand(fills[2])).astype(BF)
     own(1)[...] = masked
     row_s.start()
-    cols_[y, z] = masked
-    get_s, get_f = columns(cols_), columns(colf, 16)
+    cols_[y, z, pl.ds(0, TR), :] = masked
+    get_s, get_f = columns(cols_, 16), columns(colf)
     get_p.s2()
     row_f.forward()
     packed = jnp.zeros((16, TC), F32)
     pad16 = (iota((16, RB), 0) == iota((16, RB), 1)).astype(BF)
     for number in range(TERMS - 1):
         shift = (iota((CB, TC), 1) == CB * number + iota((CB, TC), 0)).astype(BF)
-        packed += mm(mm(pad16, seconds[number].astype(F32).astype(BF)).astype(BF), shift)
-    colf[y, z, pl.ds(TR, 16), :] = packed.astype(BF)
+        packed += mm(mm(pad16, seconds[:, number, :].astype(F32).astype(BF)).astype(BF), shift)
+    cols_[y, z, pl.ds(TR, 16), :] = packed.astype(BF)
     get_p.s3()
     row_f.near()
     row_s.forward()
@@ -276,12 +300,9 @@
     row_g.forward()
     row_g.near()
     row_h.forward()
-    row_g.far()
-    row_h.near()
-    row_h.far()
-    row_g.done()
-    row_h.done()
-
+    net.release(get_p)
+    net.release(row_f)
+    net.release(row_s)
     column_block = 24 * y + iota((1, 768), 1) // BLK
     place[...] = jnp.zeros_like(place)
 
@@ -299,13 +320,26 @@
             series[0, k, pl.ds(BLK * i, BLK), :] = hit.astype(F32).astype(BF)
         hit = jnp.logical_and(same, iota((BLK, 768), 1) // BLK + 24 * y == mine)
         filters[5, pl.ds(BLK * i, BLK), :] = hit.astype(F32).astype(BF)
-    masks[3] = expand(seconds[TERMS - 1]).astype(BF)
-    masks[4] = expand(seconds[TERMS]).astype(BF)
+    masks[3] = expand(seconds[:, TERMS - 1, :]).astype(BF)
+    masks[4] = expand(seconds[:, TERMS, :]).astype(BF)
     get_s.done()
     get_f.s2()
+    row_g.far()
+    row_h.near()
+    get_f.s3()
+    row_h.far()
+    row_g.done()
+    get_f.s4()
+    known = cols_[:, :, pl.ds(TR, 16), :].reshape(256, TC)
+    spread = iota((TC, 96), 0) - 3 * z
+    for number in range(TERMS - 1):
+        pick = (spread == CB * number + iota((TC, 96), 1) // BLK).astype(BF)
+        wide = mm(known, pick).astype(BF)
+        filters[number] = lax.dot_general(
+            wide, place[...].astype(BF), (((0,), (0,)), ((), ())), preferred_element_type=F32
+        ).astype(BF)
     product(2, cols_)
-    get_f.s3()
-    get_f.s4()
+    row_h.done()
     get_f.done()
     product(3, colf, -1)
 
@@ -324,21 +358,18 @@
     get_x.s2()
     get_x.s3()
     get_x.s4()
-    spread = (iota((16 * 24, 96), 0) - 3 * z).astype(jnp.int32)
-    known = colf[:, :, pl.ds(TR, 16), :].reshape(256, TC)
-    for number in range(TERMS - 1):
-        pick = (spread == CB * number + iota((16 * 24, 96), 1) // BLK).astype(BF)
-        wide = mm(known, pick).astype(BF)
-        filters[number] = lax.dot_general(
-            wide, place[...].astype(BF), (((0,), (0,)), ((), ())), preferred_element_type=F32
-        ).astype(BF)
     for number in (0, 4, 1, 2, 5, 6, 3, 7):
         get_x.end(number)
         pairs[number].start()
+    net.release(get_s)
+    net.release(get_f)
+    net.release(row_g)
+    net.release(row_h)
     net.wait(end)
+    net.release(get_x)
 
     def piece_times(step, k, half):
-        left = series[step, k, pl.ds(48 * half, 48), :]
+        left = series[step, k] if half is None else series[step, k, pl.ds(48 * half, 48), :]
         total = None
         for h in range(2):
             part = lax.dot_general(
@@ -349,7 +380,7 @@
         return total
 
     def filtered(step, half, total):
-        cut = pl.ds(48 * half, 48)
+        cut = pl.ds(0, 96) if half is None else pl.ds(48 * half, 48)
         eye = filters[5, cut, :].astype(F32)
         if step == 0:
             return eye + total / float(TERMS)
@@ -384,23 +415,29 @@
         series[step, y, pl.ds(48 * half, 48), :] = value.astype(BF)
 
     turns = [[Turn(step, half) for half in range(2)] for step in range(1, TERMS)]
-    for half in range(2):
-        total = piece_times(0, 0, half)
-        for k in range(1, 4):
-            total += piece_times(0, k, half)
-        put(1, half, filtered(0, half, total))
-        turns[0][half].start()
-    last = []
+    total = piece_times(0, 0, None)
+    for k in range(1, 4):
+        total += piece_times(0, k, None)
+    series[1, y] = filtered(0, None, total).astype(BF)
+    last = [None, None]
+
+    def finish(step, half):
+        value = turns[step - 1][half].finish()
+        if step < TERMS - 1:
+            put(step + 1, half, value)
+            turns[step][half].start()
+        else:
+            last[half] = value
+
+    turns[0][0].start()
+    turns[0][0].forward()
+    turns[0][1].start()
     for step in range(1, TERMS):
-        for half in range(2):
-            turns[step - 1][half].forward()
-        for half in range(2):
-            value = turns[step - 1][half].finish()
-            if step < TERMS - 1:
-                put(step + 1, half, value)
-                turns[step][half].start()
-            else:
-                last.append(value)
+        finish(step, 0)
+        turns[step - 1][1].forward()
+        if step < TERMS - 1:
+            turns[step][0].forward()
+        finish(step, 1)
 
     flat = jnp.concatenate(last, axis=0).T.astype(BF)
     for k in range(4):
@@ -435,17 +472,22 @@
     row_t = Rows(4)
     row_t.start()
     row_t.forward()
-    row_t.near()
-    row_t.far()
-    row_t.done()
     acc[...] = jnp.zeros_like(acc)
 
-    @pl.loop(0, 4)
-    def _(k):
+    def accumulate(k):
         left = rows[4, :, pl.ds(pl.multiple_of(k * 768, 768), 768)]
         right = jnp.concatenate([units[2 * order[24 * k + b] + h] for b in range(24) for h in range(2)], axis=0)
         acc[...] += mm(left, right)
 
+    net.wait(row_t.ends[0])
+    accumulate(x)
+    row_t.near()
+    net.wait(row_t.ends[1])
+    accumulate(lax.rem(x + 1, 4))
+    row_t.far()
+    accumulate(lax.rem(x + 3, 4))
+    net.wait(row_t.ends[2])
+    accumulate(lax.rem(x + 2, 4))
     value = (acc[...] * masks[3].astype(F32)).astype(BF)
     own(5)[...] = value
     colz[y, z] = value
@@ -476,8 +518,8 @@
         out_specs=vmem,
         scratch_shapes=[
             panel,
+            pltpu.VMEM((4, 4, TR + 16, TC), BF),
             panel,
-            pltpu.VMEM((4, 4, TR + 16, TC), BF),
             panel,
             panel,
             pltpu.VMEM((4, 2, 4, TR, TC), BF),
@@ -495,7 +537,7 @@
         compiler_params=pltpu.CompilerParams(
             collective_id=0, has_side_effects=True, vmem_limit_bytes=60 * 1024 * 1024
         ),
-    )(fock, density, margin, fills, firsts, seconds, owner_order)
+    )(fock, density, margin, fills, firsts, jnp.swapaxes(seconds, 0, 1), owner_order)
 
 
 def solution(mesh):

time: 170 us -> 166 us (0.976)
  Pallas kernels: 167 us -> 164 us
    pallas_call x1, Pallas kernels: 167 us -> 164 us  [on_device(): pl.pallas_call(body, out_shape=jax.ShapeDtypeStruct((TR, TC), BF), in_spe...]
where the time goes in v3:
time: 166 us
  Pallas kernels  164 us (99%)
    pallas_call x1, Pallas kernels, on_device(): pl.pallas_call(body, out_shape=jax.ShapeDtypeStruct((TR, TC), BF), in_spe...  164 us

profile of v3, /device:TPU:1, one launch (start us, length us, event | category | flops | bytes accessed | tf_op | source)
XLA Modules:
  0.0 165.5 jit_solution(8846381720888993783)
XLA Ops:
  0.0 163.9 %shard_map.73 = bf16[192,384]{1,0:T(8,128)(2,1)} custom-call(bf16[192,384]{1,0:T(8,128)(2,1)} %fock.1, bf16[192,384]{1,0:T(8,128)(2,1)} %density.1, bf16[192,384]{1,0:T(8,128)(2,1)} %margin.1, s32[3,6,12]{2,1,0:T(8,128)} %fills.1, s32[3,6,12]{2,1,0:T(8,128)} %firsts.1, s32[6,7,12]{2,1,0:T(8,128)} %bitcast.1, s32[96]{0:T(128)} %order.1), custom_call_target="tpu_custom_call" | custom-call | tf_op jit(solution)/shard_map/pallas_call | solution.py:514
  163.9 1.6 copy.9

commit v4 on v3

--- a/solution.py
+++ b/solution.py
@@ -163,7 +163,7 @@
 
 def body(
     fock, density, margin, fills, firsts, seconds, order, out,
-    colp, cols_, colf, colt, colz, panel, series, units, rows, acc, masks, filters, place, turned, arrived, sems,
+    colp, cols_, colf, colt, colz, panel, series, units, rows, acc, masks, filters, place, sems,
 ):
     r, c = lax.axis_index("row"), lax.axis_index("col")
     y, z = r // 4, lax.rem(r, 4)
@@ -176,13 +176,12 @@
     next_y = (dev(y + 1, z, x), dev(y - 1, z, x))
     next_z = (dev(y, z + 1, x), dev(y, z - 1, x))
     next_x = (dev(y, z, x + 1), dev(y, z, x - 1))
-    across = dev(y, z + 2, x)
     sibling = (r, 2 * x + 1 - core)
 
     barrier = pltpu.get_barrier_semaphore()
-    for device in next_y + next_z + next_x + (across, sibling):
+    for device in next_y + next_z + next_x + (sibling,):
         pl.semaphore_signal(barrier, inc=1, device_id=device, device_id_type=MESH)
-    pl.semaphore_wait(barrier, 8)
+    pl.semaphore_wait(barrier, 7)
 
     def columns(buf, extra=0):
         parts = ((0, 48), (48, 48)), ((96, 48), (144, 48 + extra))
@@ -342,18 +341,23 @@
     row_h.done()
     get_f.done()
     product(3, colf, -1)
+    net.release(get_s)
+    net.release(get_f)
+    net.release(row_g)
+    net.release(row_h)
 
     tile = (acc[...] * masks[2].astype(F32)).astype(BF)
-    panel[x, core, z] = (tile.astype(F32) * 0.25).astype(BF)
-    cut = lambda base: lambda k1, k2, p: panel.at[k2, core, k1, pl.ds(base + 48 * p, 48), :]
+    side = pl.ds(pl.multiple_of(core * TC, TC), TC)
+    panel[x, z, :, side] = (tile.astype(F32) * 0.25).astype(BF)
+    cut = lambda base: lambda k1, k2, p: panel.at[k2, k1, pl.ds(base + 48 * p, 48), side]
     get_x = Plane(net, z, next_z, x, next_x, cut(0), cut(96), (3, 3), (3, 3))
     get_x.s1()
     sent, pairs, end = net.senders(), [], net.group()
     for s in (0, -1, 1, 2):
-        ref = panel.at[:, core, lax.rem(z + s + 4, 4), pl.ds(0, 96), :]
+        ref = panel.at[:, lax.rem(z + s + 4, 4), pl.ds(0, 96), side]
         pairs.append(net.copy(ref, sibling, sent, 24, end))
     for s in (0, -1, 1, 2):
-        ref = panel.at[lax.rem(x + s + 4, 4), core, :, pl.ds(96, 96), :]
+        ref = panel.at[lax.rem(x + s + 4, 4), :, pl.ds(96, 96), side]
         pairs.append(net.copy(ref, sibling, sent, 24, end))
     get_x.s2()
     get_x.s3()
@@ -361,23 +365,14 @@
     for number in (0, 4, 1, 2, 5, 6, 3, 7):
         get_x.end(number)
         pairs[number].start()
-    net.release(get_s)
-    net.release(get_f)
-    net.release(row_g)
-    net.release(row_h)
     net.wait(end)
     net.release(get_x)
 
     def piece_times(step, k, half):
         left = series[step, k] if half is None else series[step, k, pl.ds(48 * half, 48), :]
-        total = None
-        for h in range(2):
-            part = lax.dot_general(
-                left[:, TC * h : TC * (h + 1)], panel[k, h].reshape(768, TC),
-                (((1,), (1,)), ((), ())), preferred_element_type=F32,
-            )
-            total = part if total is None else total + part
-        return total
+        return lax.dot_general(
+            left, panel[k].reshape(768, 768), (((1,), (1,)), ((), ())), preferred_element_type=F32
+        )
 
     def filtered(step, half, total):
         cut = pl.ds(0, 96) if half is None else pl.ds(48 * half, 48)
@@ -400,13 +395,14 @@
         def forward(self):
             self.ring.forward()
 
+        def middle(self):
+            net.wait(self.near)
+            for s in (-1, 1):
+                sums[self.half] += piece_times(self.step, lax.rem(y + s + 4, 4), self.half)
+
         def finish(self):
-            net.wait(self.near)
-            total = sums[self.half]
-            for s in (-1, 1):
-                total += piece_times(self.step, lax.rem(y + s + 4, 4), self.half)
             net.wait(self.far)
-            total += piece_times(self.step, lax.rem(y + 2, 4), self.half)
+            total = sums[self.half] + piece_times(self.step, lax.rem(y + 2, 4), self.half)
             return filtered(self.step, self.half, total)
 
     sums = {}
@@ -419,7 +415,8 @@
     for k in range(1, 4):
         total += piece_times(0, k, None)
     series[1, y] = filtered(0, None, total).astype(BF)
-    last = [None, None]
+    cut = lambda base: lambda k1, k2, p: colt.at[k2, k1, pl.ds(base, 48), pl.ds(TC * p, TC)]
+    get_t = Plane(net, z, next_z, y, next_y, cut(0), cut(48), (3, 3), (3, 3))
 
     def finish(step, half):
         value = turns[step - 1][half].finish()
@@ -427,44 +424,28 @@
             put(step + 1, half, value)
             turns[step][half].start()
         else:
-            last[half] = value
+            colt[y, z, pl.ds(48 * half, 48), :] = value.astype(BF)
+            for ring in ((get_t.a1, get_t.a2[0]), (get_t.b1, get_t.b2[0]))[half]:
+                ring.start()
 
     turns[0][0].start()
+    turns[0][1].start()
     turns[0][0].forward()
-    turns[0][1].start()
     for step in range(1, TERMS):
+        turns[step - 1][0].middle()
+        turns[step - 1][1].forward()
         finish(step, 0)
-        turns[step - 1][1].forward()
+        turns[step - 1][1].middle()
         if step < TERMS - 1:
             turns[step][0].forward()
         finish(step, 1)
 
-    flat = jnp.concatenate(last, axis=0).T.astype(BF)
-    for k in range(4):
-        turned[k] = flat[TR * k : TR * (k + 1), :]
-    made = []
-    for s, device in ((1, next_z[0]), (-1, next_z[1]), (2, across)):
-        made.append(net.copy(turned.at[lax.rem(z + s + 4, 4)], device, [net.sem(), 0], 0, None, arrived.at[z]))
-    for copy in made:
-        copy.start()
-    arrived[z] = turned[z]
-    for copy in made:
-        copy.wait()
-    value = jnp.zeros((TR, TC), F32)
-    for k in range(4):
-        lane = (iota((96, TC), 0) + 96 * k == iota((96, TC), 1)).astype(BF)
-        value += mm(arrived[k], lane)
-    colt[y, z] = value.astype(BF)
-    get_t = columns(colt)
-    get_t.s1()
     get_t.s2()
     get_t.s3()
     get_t.s4()
     get_t.done()
-
-    @pl.loop(0, 4)
-    def _(k):
-        units[pl.ds(48 * k, 48)] = colt[k].reshape(48, 16, TC)
+    for k in range(4):
+        units[pl.ds(48 * k, 48)] = colt[k].reshape(TC, 768).T.reshape(48, 16, TC)
 
     for b in range(RB):
         for h in range(2):
@@ -520,9 +501,9 @@
             panel,
             pltpu.VMEM((4, 4, TR + 16, TC), BF),
             panel,
+            pltpu.VMEM((4, 4, 96, 768), BF),
             panel,
-            panel,
-            pltpu.VMEM((4, 2, 4, TR, TC), BF),
+            pltpu.VMEM((4, 4, TR, 768), BF),
             pltpu.VMEM((TERMS, 4, 96, 768), BF),
             pltpu.VMEM((192, 16, TC), BF),
             pltpu.VMEM((6, TR, N), BF),
@@ -530,8 +511,6 @@
             pltpu.VMEM((5, TR, TC), BF),
             pltpu.VMEM((6, 96, 768), BF),
             pltpu.VMEM((256, 768), F32),
-            pltpu.VMEM((4, TR, 96), BF),
-            pltpu.VMEM((4, TR, 96), BF),
             pltpu.SemaphoreType.DMA((SEMS,)),
         ],
         compiler_params=pltpu.CompilerParams(

time: 166 us -> 160 us (0.964)
  Pallas kernels: 164 us -> 158 us
    pallas_call x1, Pallas kernels: 164 us -> 158 us  [on_device(): pl.pallas_call(body, out_shape=jax.ShapeDtypeStruct((TR, TC), BF), in_spe...]
where the time goes in v4:
time: 160 us; the launch traced here: 159 us
  Pallas kernels  158 us (99%)
    pallas_call x1, Pallas kernels, on_device(): pl.pallas_call(body, out_shape=jax.ShapeDtypeStruct((TR, TC), BF), in_spe...  158 us

profile of v4, /device:TPU:1, one launch (start us, length us, event | category | flops | bytes accessed | tf_op | source)
XLA Modules:
  0.0 159.5 jit_solution(3842074421171412234)
XLA Ops:
  0.0 157.9 %shard_map.73 = bf16[192,384]{1,0:T(8,128)(2,1)} custom-call(bf16[192,384]{1,0:T(8,128)(2,1)} %fock.1, bf16[192,384]{1,0:T(8,128)(2,1)} %density.1, bf16[192,384]{1,0:T(8,128)(2,1)} %margin.1, s32[3,6,12]{2,1,0:T(8,128)} %fills.1, s32[3,6,12]{2,1,0:T(8,128)} %firsts.1, s32[6,7,12]{2,1,0:T(8,128)} %bitcast.1, s32[96]{0:T(128)} %order.1), custom_call_target="tpu_custom_call" | custom-call | tf_op jit(solution)/shard_map/pallas_call | solution.py:495
  157.9 1.6 copy.9

commit v5 on v4

--- a/solution.py
+++ b/solution.py
@@ -163,7 +163,7 @@
 
 def body(
     fock, density, margin, fills, firsts, seconds, order, out,
-    colp, cols_, colf, colt, colz, panel, series, units, rows, acc, masks, filters, place, sems,
+    colp, cols_, colf, colt, colz, panel, series, units, rows, acc, masks, filters, place, across, sems,
 ):
     r, c = lax.axis_index("row"), lax.axis_index("col")
     y, z = r // 4, lax.rem(r, 4)
@@ -370,9 +370,7 @@
 
     def piece_times(step, k, half):
         left = series[step, k] if half is None else series[step, k, pl.ds(48 * half, 48), :]
-        return lax.dot_general(
-            left, panel[k].reshape(768, 768), (((1,), (1,)), ((), ())), preferred_element_type=F32
-        )
+        return mm(left, across[k])
 
     def filtered(step, half, total):
         cut = pl.ds(0, 96) if half is None else pl.ds(48 * half, 48)
@@ -411,9 +409,11 @@
         series[step, y, pl.ds(48 * half, 48), :] = value.astype(BF)
 
     turns = [[Turn(step, half) for half in range(2)] for step in range(1, TERMS)]
-    total = piece_times(0, 0, None)
-    for k in range(1, 4):
-        total += piece_times(0, k, None)
+    total = jnp.zeros((96, 768), F32)
+    for k in range(4):
+        block = panel[k].reshape(768, 768).T
+        across[k] = block
+        total += mm(series[0, k], block)
     series[1, y] = filtered(0, None, total).astype(BF)
     cut = lambda base: lambda k1, k2, p: colt.at[k2, k1, pl.ds(base, 48), pl.ds(TC * p, TC)]
     get_t = Plane(net, z, next_z, y, next_y, cut(0), cut(48), (3, 3), (3, 3))
@@ -430,15 +430,12 @@
 
     turns[0][0].start()
     turns[0][1].start()
-    turns[0][0].forward()
     for step in range(1, TERMS):
-        turns[step - 1][0].middle()
-        turns[step - 1][1].forward()
-        finish(step, 0)
-        turns[step - 1][1].middle()
-        if step < TERMS - 1:
-            turns[step][0].forward()
-        finish(step, 1)
+        for half in range(2):
+            turns[step - 1][half].forward()
+        for half in range(2):
+            turns[step - 1][half].middle()
+            finish(step, half)
 
     get_t.s2()
     get_t.s3()
@@ -452,13 +449,19 @@
             own(4)[pl.ds(BLK * b + 16 * h, 16), :] = units[2 * order[r * RB + b] + h]
     row_t = Rows(4)
     row_t.start()
+
+    @pl.loop(0, 4)
+    def _(k):
+        for b in range(24):
+            for h in range(2):
+                colf[k, b // 6, pl.ds(BLK * (b % 6) + 16 * h, 16), :] = units[2 * order[24 * k + b] + h]
+
     row_t.forward()
     acc[...] = jnp.zeros_like(acc)
 
     def accumulate(k):
         left = rows[4, :, pl.ds(pl.multiple_of(k * 768, 768), 768)]
-        right = jnp.concatenate([units[2 * order[24 * k + b] + h] for b in range(24) for h in range(2)], axis=0)
-        acc[...] += mm(left, right)
+        acc[...] += mm(left, colf[k].reshape(768, TC))
 
     net.wait(row_t.ends[0])
     accumulate(x)
@@ -511,6 +514,7 @@
             pltpu.VMEM((5, TR, TC), BF),
             pltpu.VMEM((6, 96, 768), BF),
             pltpu.VMEM((256, 768), F32),
+            pltpu.VMEM((4, 768, 768), BF),
             pltpu.SemaphoreType.DMA((SEMS,)),
         ],
         compiler_params=pltpu.CompilerParams(

time: 160 us -> 153 us (0.956)
  Pallas kernels: 158 us -> 151 us
    pallas_call x1, Pallas kernels: 158 us -> 151 us  [on_device(): pl.pallas_call(body, out_shape=jax.ShapeDtypeStruct((TR, TC), BF), in_spe...]
where the time goes in v5:
time: 153 us
  Pallas kernels  151 us (99%)
  local copies, waits for them, and re-layouts  1.59 us (1%)
    pallas_call x1, Pallas kernels, on_device(): pl.pallas_call(body, out_shape=jax.ShapeDtypeStruct((TR, TC), BF), in_spe...  151 us

profile of v5, /device:TPU:1, one launch (start us, length us, event | category | flops | bytes accessed | tf_op | source)
XLA Modules:
  0.0 152.7 jit_solution(8477270278004397724)
XLA Ops:
  0.0 151.1 %shard_map.73 = bf16[192,384]{1,0:T(8,128)(2,1)} custom-call(bf16[192,384]{1,0:T(8,128)(2,1)} %fock.1, bf16[192,384]{1,0:T(8,128)(2,1)} %density.1, bf16[192,384]{1,0:T(8,128)(2,1)} %margin.1, s32[3,6,12]{2,1,0:T(8,128)} %fills.1, s32[3,6,12]{2,1,0:T(8,128)} %firsts.1, s32[6,7,12]{2,1,0:T(8,128)} %bitcast.1, s32[96]{0:T(128)} %order.1), custom_call_target="tpu_custom_call" | custom-call | tf_op jit(solution)/shard_map/pallas_call | solution.py:498
  151.1 1.6 %copy.9 = bf16[192,384]{1,0:T(8,128)(2,1)} copy(bf16[192,384]{1,0:T(8,128)(2,1)} %shard_map.73) | data formatting | bytes 294912

commit v6 on v5

--- a/solution.py
+++ b/solution.py
@@ -105,7 +105,7 @@
 
 
 class Plane:
-    def __init__(self, net, k1, next1, k2, next2, piece_a, piece_b, sizes_a, sizes_b):
+    def __init__(self, net, k1, next1, k2, next2, piece_a, piece_b, sizes_a, sizes_b, fine=False):
         self.net = net
         net.taken = []
         sends = [net.senders(), net.senders()]
@@ -116,9 +116,10 @@
         def second(k, nexts, piece, sizes, sent):
             rings = []
             for s in steps:
-                end = net.group()
-                self.ends.append(end)
-                rings.append(Ring(net, k, nexts, piece(s), sizes, sent, end, end))
+                near = net.group()
+                far = net.group() if fine and s == 2 else near
+                self.ends.append((near, far))
+                rings.append(Ring(net, k, nexts, piece(s), sizes, sent, near, far))
             return rings
 
         self.a1 = Ring(net, k1, next1, lambda k, p: piece_a(k, k2, p), sizes_a, sends[0])
@@ -154,7 +155,7 @@
             self.b2[number].forward()
 
     def end(self, number):
-        self.net.wait(self.ends[number])
+        self.net.wait(self.ends[number][0])
 
     def done(self):
         for number in range(8):
@@ -181,7 +182,6 @@
     barrier = pltpu.get_barrier_semaphore()
     for device in next_y + next_z + next_x + (sibling,):
         pl.semaphore_signal(barrier, inc=1, device_id=device, device_id_type=MESH)
-    pl.semaphore_wait(barrier, 7)
 
     def columns(buf, extra=0):
         parts = ((0, 48), (48, 48)), ((96, 48), (144, 48 + extra))
@@ -253,13 +253,14 @@
                 acc[...] += mm(left, right)
 
     colp[y, z] = (density[...].astype(F32) * expand(fills[1])).astype(BF)
+    masked = (fock[...].astype(F32) * expand(fills[0])).astype(BF)
+    own(0)[...] = masked
+    colf[y, z] = masked
+    pl.semaphore_wait(barrier, 7)
     get_p = columns(colp)
     get_p.s1()
     row_f, row_s, row_g, row_h = [Rows(number) for number in range(4)]
-    masked = (fock[...].astype(F32) * expand(fills[0])).astype(BF)
-    own(0)[...] = masked
     row_f.start()
-    colf[y, z] = masked
     masked = (margin[...].astype(F32) * expand(fills[2])).astype(BF)
     own(1)[...] = masked
     row_s.start()
@@ -350,21 +351,35 @@
     side = pl.ds(pl.multiple_of(core * TC, TC), TC)
     panel[x, z, :, side] = (tile.astype(F32) * 0.25).astype(BF)
     cut = lambda base: lambda k1, k2, p: panel.at[k2, k1, pl.ds(base + 48 * p, 48), side]
-    get_x = Plane(net, z, next_z, x, next_x, cut(0), cut(96), (3, 3), (3, 3))
+    get_x = Plane(net, z, next_z, x, next_x, cut(0), cut(96), (3, 3), (3, 3), True)
     get_x.s1()
     sent, pairs, end = net.senders(), [], net.group()
+    turn = lambda k, s: lax.rem(k + s + 4, 4)
+    for s in (0, -1, 1):
+        ref = panel.at[:, turn(z, s), pl.ds(0, 96), side]
+        pairs.append(net.copy(ref, sibling, sent, 24, end))
+    for s in (0, -1, 1):
+        ref = panel.at[turn(x, s), :, pl.ds(96, 96), side]
+        pairs.append(net.copy(ref, sibling, sent, 24, end))
+    tails = [[], []]
     for s in (0, -1, 1, 2):
-        ref = panel.at[:, lax.rem(z + s + 4, 4), pl.ds(0, 96), side]
-        pairs.append(net.copy(ref, sibling, sent, 24, end))
-    for s in (0, -1, 1, 2):
-        ref = panel.at[lax.rem(x + s + 4, 4), :, pl.ds(96, 96), side]
-        pairs.append(net.copy(ref, sibling, sent, 24, end))
+        ref = panel.at[turn(x, s), turn(z, 2), pl.ds(0, 96), side]
+        tails[0].append(net.copy(ref, sibling, sent, 6, end))
+        ref = panel.at[turn(x, 2), turn(z, s), pl.ds(96, 96), side]
+        tails[1].append(net.copy(ref, sibling, sent, 6, end))
     get_x.s2()
     get_x.s3()
+    for tail in tails:
+        tail[0].start()
     get_x.s4()
-    for number in (0, 4, 1, 2, 5, 6, 3, 7):
+    for number, pair in ((0, 0), (4, 3), (1, 1), (2, 2), (5, 4), (6, 5)):
         get_x.end(number)
-        pairs[number].start()
+        pairs[pair].start()
+    for part in range(2):
+        for number, tail in ((3, tails[0]), (7, tails[1])):
+            net.wait(get_x.ends[number][part])
+            for copy in ((tail[1], tail[2]), (tail[3],))[part]:
+                copy.start()
     net.wait(end)
     net.release(get_x)
 

time: 153 us -> 152 us (level)
  no operation moved by 1% of the time
where the time goes in v6:
time: 152 us
  Pallas kernels  151 us (99%)
  local copies, waits for them, and re-layouts  1.59 us (1%)
    pallas_call x1, Pallas kernels, on_device(): pl.pallas_call(body, out_shape=jax.ShapeDtypeStruct((TR, TC), BF), in_spe...  151 us

profile of v6, /device:TPU:1, one launch (start us, length us, event | category | flops | bytes accessed | tf_op | source)
XLA Modules:
  0.0 152.2 jit_solution(3652285158627546183)
XLA Ops:
  0.0 150.6 %shard_map.73 = bf16[192,384]{1,0:T(8,128)(2,1)} custom-call(bf16[192,384]{1,0:T(8,128)(2,1)} %fock.1, bf16[192,384]{1,0:T(8,128)(2,1)} %density.1, bf16[192,384]{1,0:T(8,128)(2,1)} %margin.1, s32[3,6,12]{2,1,0:T(8,128)} %fills.1, s32[3,6,12]{2,1,0:T(8,128)} %firsts.1, s32[6,7,12]{2,1,0:T(8,128)} %bitcast.1, s32[96]{0:T(128)} %order.1), custom_call_target="tpu_custom_call" | custom-call | tf_op jit(solution)/shard_map/pallas_call | solution.py:513
  150.6 1.6 %copy.9 = bf16[192,384]{1,0:T(8,128)(2,1)} copy(bf16[192,384]{1,0:T(8,128)(2,1)} %shard_map.73) | data formatting | bytes 294912

commit v7 on v6

--- a/solution.py
+++ b/solution.py
@@ -403,7 +403,6 @@
 
         def start(self):
             self.ring.start()
-            sums[self.half] = piece_times(self.step, y, self.half)
 
         def forward(self):
             self.ring.forward()
@@ -426,9 +425,9 @@
     turns = [[Turn(step, half) for half in range(2)] for step in range(1, TERMS)]
     total = jnp.zeros((96, 768), F32)
     for k in range(4):
-        block = panel[k].reshape(768, 768).T
-        across[k] = block
-        total += mm(series[0, k], block)
+        total += lax.dot_general(
+            series[0, k], panel[k].reshape(768, 768), (((1,), (1,)), ((), ())), preferred_element_type=F32
+        )
     series[1, y] = filtered(0, None, total).astype(BF)
     cut = lambda base: lambda k1, k2, p: colt.at[k2, k1, pl.ds(base, 48), pl.ds(TC * p, TC)]
     get_t = Plane(net, z, next_z, y, next_y, cut(0), cut(48), (3, 3), (3, 3))
@@ -445,9 +444,13 @@
 
     turns[0][0].start()
     turns[0][1].start()
+    for k in range(4):
+        across[k] = panel[k].reshape(768, 768).T
     for step in range(1, TERMS):
         for half in range(2):
             turns[step - 1][half].forward()
+        own_part = piece_times(step, y, None)
+        sums[0], sums[1] = own_part[:48, :], own_part[48:, :]
         for half in range(2):
             turns[step - 1][half].middle()
             finish(step, half)

time: 152 us -> 153 us (level)
  no operation moved by 1% of the time
where the time goes in v7:
time: 153 us
  Pallas kernels  151 us (99%)
  local copies, waits for them, and re-layouts  1.59 us (1%)
    pallas_call x1, Pallas kernels, on_device(): pl.pallas_call(body, out_shape=jax.ShapeDtypeStruct((TR, TC), BF), in_spe...  151 us

profile of v7, /device:TPU:1, one launch (start us, length us, event | category | flops | bytes accessed | tf_op | source)
XLA Modules:
  0.0 152.6 jit_solution(14665779265898457871)
XLA Ops:
  0.0 151.0 %shard_map.73 = bf16[192,384]{1,0:T(8,128)(2,1)} custom-call(bf16[192,384]{1,0:T(8,128)(2,1)} %fock.1, bf16[192,384]{1,0:T(8,128)(2,1)} %density.1, bf16[192,384]{1,0:T(8,128)(2,1)} %margin.1, s32[3,6,12]{2,1,0:T(8,128)} %fills.1, s32[3,6,12]{2,1,0:T(8,128)} %firsts.1, s32[6,7,12]{2,1,0:T(8,128)} %bitcast.1, s32[96]{0:T(128)} %order.1), custom_call_target="tpu_custom_call" | custom-call | tf_op jit(solution)/shard_map/pallas_call | solution.py:516
  151.0 1.6 %copy.9 = bf16[192,384]{1,0:T(8,128)(2,1)} copy(bf16[192,384]{1,0:T(8,128)(2,1)} %shard_map.73) | data formatting | bytes 294912
